TPU v7x, 32 devices: a whole 2x2x4 slice. The times are simulated.
32 devices in a mesh: groups: 2 (over y), state: 4 (over z), type: 4 (over x, core).
Axes of the slice: x: 2, y: 2, z: 4, core: 2. Of those that a mesh axis runs over, the one named last changes fastest.
Arguments:
- value_in: bfloat16 [16384, 2048], P(('groups', 'state'), 'type'), parts along dimension 0, may hold values from -7.5 to 7.5
- cotangent: bfloat16 [16384, 2048], P(('groups', 'state'), 'type'), parts along dimension 0, may hold values from -100 to 100
- state_util: float32 [2, 16384], P(None, ('groups', 'state')), parts along dimension 1, may hold values from -300 to 300
- taste: float32 [2, 4096], P(None, ('groups', 'type')), parts along dimension 1, may hold values from -6 to 6
- tiles: bfloat16 [128, 2, 6, 128, 128], P(('groups', 'state')), parts along dimension 0, may hold values from 0 to 0.0051879883
- dest_block: int32 [128, 2, 6], P(('groups', 'state')), parts along dimension 0, may hold values from 0 to 63, as said below
- counts: int32 [128, 2], P(('groups', 'state')), parts along dimension 0, may hold values from 1 to 6
Outputs:
- value_out: float32 [16384, 2048], P(('groups', 'state'), 'type'), parts along dimension 0
- adjoint: float32 [16384, 2048], P(('groups', 'state'), 'type'), parts along dimension 0
- grad_util: float32 [2, 16384], P(None, ('groups', 'state')), parts along dimension 1
- grad_taste: float32 [2, 4096], P(None, ('groups', 'type')), parts along dimension 1
There are 2 independent parts, one for each index of `groups`. A program takes and returns all parts, laid end to end along the dimension named above; each array names one. Nothing has to cross between parts.
Inputs may be any that keep to these rules, and one draw needn't show every extreme that they name: `dest_block`: entries at or beyond a list's count name blocks of the list's own run of 16 blocks. In each run of 16 blocks exactly 16 used entries name blocks outside the run, at most 6 of them in any one other run, and exactly 6 in some other run.
All inputs are finite; a program needn't handle non-finite values.
Results may differ from a plain program's by a relative error of at most 0.0012.
Values may be sent and summed in bfloat16 or wider, within the bound.
A program may use at most 192 MiB of HBM per device.

v0:
```python
import jax
import jax.numpy as jnp
from jax import lax
from jax.sharding import PartitionSpec as P


def local(value_in, cotangent, state_util, taste, tiles, dest_block, counts):
    block_count, action_count, entry_count, tile_rows, _ = tiles.shape
    type_width = value_in.shape[1]
    device_count = lax.axis_size("state")
    my_index = lax.axis_index("state")
    capacity = max(2, (block_count + device_count - 2) // (device_count - 1))
    entry_total = block_count * action_count * entry_count
    value_blocks = value_in.reshape(block_count, tile_rows, type_width)
    flat_dest = dest_block.reshape(entry_total)
    owner = flat_dest // block_count
    local_block = flat_dest % block_count
    used = (jnp.arange(entry_count, dtype=jnp.int32)[None, None, :] < counts[:, :, None]).reshape(
        entry_total
    )
    remote = used & (owner != my_index)
    local_used = used & (owner == my_index)
    peer_ids = jnp.arange(device_count, dtype=jnp.int32)
    owner_hits = (remote[:, None] & (owner[:, None] == peer_ids[None, :])).astype(jnp.int32)
    earlier = jnp.cumsum(owner_hits, axis=0) - owner_hits
    slot_of = jnp.sum(earlier * owner_hits, axis=1)
    target = jnp.where(remote, owner * capacity + slot_of, device_count * capacity)
    request = (
        jnp.full((device_count * capacity,), -1, jnp.int32).at[target].set(local_block, mode="drop")
    )
    source_entry = (
        jnp.full((device_count * capacity,), -1, jnp.int32)
        .at[target]
        .set(jnp.arange(entry_total, dtype=jnp.int32), mode="drop")
    )
    wanted = lax.all_to_all(
        request.reshape(device_count, capacity), "state", split_axis=0, concat_axis=0, tiled=True
    )
    outgoing = jnp.take(value_blocks, jnp.clip(wanted.reshape(-1), 0, block_count - 1), axis=0)
    incoming = lax.all_to_all(
        outgoing.reshape(device_count, capacity, tile_rows, type_width),
        "state",
        split_axis=0,
        concat_axis=0,
        tiled=True,
    )
    table = jnp.concatenate(
        [value_blocks, incoming.reshape(device_count * capacity, tile_rows, type_width)], axis=0
    )
    lookup = jnp.where(remote, block_count + target, local_block)
    picked = jnp.take(table, lookup, axis=0)
    picked = jnp.where(used[:, None, None], picked, jnp.zeros_like(picked))
    picked = picked.reshape(block_count, action_count, entry_count, tile_rows, type_width)
    cont = jnp.einsum("bamij,bamjk->baik", tiles, picked, preferred_element_type=jnp.float32)
    util_grid = state_util.reshape(action_count, block_count, tile_rows).transpose(1, 0, 2)[
        :, :, :, None
    ]
    scores = util_grid + taste[None, :, None, :] + 0.95 * cont
    largest = jnp.max(scores, axis=1)
    value = largest + jnp.log(jnp.sum(jnp.exp(scores - largest[:, None]), axis=1))
    prob = jnp.exp(scores - value[:, None])
    grad_q = cotangent.reshape(block_count, 1, tile_rows, type_width).astype(jnp.float32) * prob
    util_part = (
        jnp.sum(grad_q, axis=3).transpose(1, 0, 2).reshape(action_count, block_count * tile_rows)
    )
    util_total = lax.psum(util_part, "type") / (type_width * lax.axis_size("type"))
    taste_total = lax.psum(jnp.sum(grad_q, axis=(0, 2)), "state") / (
        block_count * tile_rows * device_count
    )
    scaled = (0.95 * grad_q).astype(jnp.bfloat16)
    slot_valid = source_entry >= 0
    safe_entry = jnp.clip(source_entry, 0, entry_total - 1)
    contrib = jnp.einsum(
        "bamij,baik->bamjk", tiles, scaled, preferred_element_type=jnp.float32
    ).reshape(entry_total, tile_rows, type_width)
    outbound = jnp.where(
        slot_valid[:, None, None], jnp.take(contrib, safe_entry, axis=0), 0.0
    ).astype(jnp.bfloat16)
    returned = lax.all_to_all(
        outbound.reshape(device_count, capacity, tile_rows, type_width),
        "state",
        split_axis=0,
        concat_axis=0,
        tiled=True,
    )
    block_ids = jnp.arange(block_count, dtype=jnp.int32)
    local_select = (local_used[:, None] & (local_block[:, None] == block_ids[None, :])).astype(
        jnp.float32
    )
    own_terms = jnp.einsum("rd,rjk->djk", local_select, contrib, precision=lax.Precision.HIGHEST)
    arrive_select = (wanted.reshape(-1)[None, :] == block_ids[:, None]).astype(jnp.bfloat16)
    arrived = jnp.dot(
        arrive_select,
        returned.reshape(device_count * capacity, tile_rows * type_width),
        preferred_element_type=jnp.float32,
    )
    adjoint = own_terms + arrived.reshape(block_count, tile_rows, type_width)
    value_out = value.reshape(block_count * tile_rows, type_width)
    return (
        value_out,
        adjoint.reshape(block_count * tile_rows, type_width),
        util_total,
        taste_total,
    )


def solution(mesh):
    return jax.shard_map(
        local,
        mesh=mesh,
        in_specs=(
            P(("groups", "state"), "type"),
            P(("groups", "state"), "type"),
            P(None, ("groups", "state")),
            P(None, ("groups", "type")),
            P(("groups", "state"), None, None, None, None),
            P(("groups", "state"), None, None),
            P(("groups", "state"), None),
        ),
        out_specs=(
            P(("groups", "state"), "type"),
            P(("groups", "state"), "type"),
            P(None, ("groups", "state")),
            P(None, ("groups", "type")),
        ),
        check_vma=False,
    )
```

profile of v0, /device:TPU:0, one launch (start us, length us, event | category | flops | bytes accessed | tf_op | source)
XLA Modules:
  0.0 337.9 jit_solution(11441029719686296648)
XLA Ops:
  0.6 0.8 copy.37
  1.4 0.1 iota_compare_fusion.1
  1.5 0.1 lt.106
  1.6 0.1 lt.109
  1.7 0.8 copy.38
  2.5 0.1 reshape.392
  2.6 0.1 reshape.396
  2.8 1.2 reduce-window.6
  4.1 0.1 copy.43
  4.3 0.1 copy.44
  4.5 1.2 scatter_custom_fusion
  5.7 0.1 all_to_all.12
  5.8 11.7 %all_to_all.19 = s32[4,1,6]{2,1,0:T(1,128)S(1)} all-to-all(s32[4,1,6]{2,1,0:T(1,128)S(1)} %bitcast.86), channel_id=1, replica_groups=mesh['groups'=2,'state'=4,'type'=4] {'state'}, dimensions={0} | all-to-all | bytes 192 | tf_op jit(solution)/shard_map/all_to_all | solution.py:36
  17.5 0.5 broadcast.505
  18.0 0.7 fusion.47
  18.7 0.1 min.24
  18.8 2.3 gather_fusion
  21.1 2.0 broadcast_select_fusion
  23.2 4.8 %all-to-all-start.1 = ((bf16[4,6,128,512]{3,2,1,0:T(8,128)(2,1)}), bf16[4,6,128,512]{3,2,1,0:T(8,128)(2,1)}, u32[]{:S(2)}, u32[]{:S(2)}) async-start(bf16[4,6,128,512]{3,2,1,0:T(8,128)(2,1)} %broadcast_select_fusion), calls=%async_computation.1 | async-start | bytes 6291456 | tf_op jit(solution)/shard_map/all_to_all | solution.py:40
  28.0 0.1 reduce_sum.41
  28.1 1.4 scatter_custom_fusion.1
  29.5 0.1 broadcast_in_dim.91
  29.6 0.1 broadcast_in_dim.89
  29.7 4.1 %copy.49 = f32[16,128,512]{1,2,0:T(8,128)} copy(bf16[16,128,512]{2,1,0:T(8,128)(2,1)} %bitcast.81) | data formatting | bytes 6291456 | tf_op jit(solution)/shard_map/convert_element_type | solution.py:62
  33.8 0.1 compare_and_fusion
  33.9 63.7 %all-to-all-done.1 = bf16[4,6,128,512]{3,2,1,0:T(8,128)(2,1)} async-done(((bf16[4,6,128,512]{3,2,1,0:T(8,128)(2,1)}), bf16[4,6,128,512]{3,2,1,0:T(8,128)(2,1)}, u32[]{:S(2)}, u32[]{:S(2)}) %all-to-all-start.1) | async-done | bytes 3145760 | tf_op jit(solution)/shard_map/all_to_all | solution.py:40
  97.5 4.7 %pad_maximum_fusion = bf16[40,128,512]{2,1,0:T(8,128)(2,1)} fusion(bf16[24,128,512]{2,1,0:T(8,128)(2,1)} %bitcast.11, bf16[16,128,512]{2,1,0:T(8,128)(2,1)S(1)} %bitcast.75), kind=kLoop, calls=%fused_computation.20 | loop fusion | flops 2621440 | bytes 10485760 | tf_op jit(solution)/shard_map/concatenate | solution.py:47
  102.3 13.6 %gather_fusion.1 = bf16[192,128,512]{2,1,0:T(8,128)(2,1)} fusion(bf16[40,128,512]{2,1,0:T(8,128)(2,1)} %pad_maximum_fusion, s32[1024]{0:T(1024)S(1)} %pad_clamp_fusion.1), kind=kCustom, calls=%fused_computation.1 | custom fusion | bytes 50332416 | tf_op jit(solution)/shard_map/jit(_take)/gather | solution.py:51
  115.8 32.6 %copy.47 = bf16[16,2,6,128,512]{3,4,2,1,0:T(8,128)(2,1)} copy(bf16[16,2,6,128,512]{4,3,2,1,0:T(8,128)(2,1)} %bitcast.73) | data formatting | bytes 50331648 | tf_op jit(solution)/shard_map/jit(_take)/gather | solution.py:51
  148.4 15.0 %fusion.48 = (f32[16,128,512]{1,2,0:T(8,128)}, f32[16,2,128,512]{2,3,1,0:T(8,128)S(1)}) fusion(bf16[16,2,6,128,128]{4,3,2,1,0:T(8,128)(2,1)} %param.11, bf16[16,2,6,128,512]{3,4,2,1,0:T(8,128)(2,1)} %copy.47, pred[16,2,6]{2,1,0:T(4,128)(4,1)S(1)} %compare_and_fusion, pred[16,2,6]{2,1,0:T(4,128)(4,1)S(1)} %iota_compare_fusion.1, ...), kind=kOutput, calls=%fused_computation.102 | convolution fusion | flops 3253731328 | bytes 44061056 | tf_op jit(solution)/shard_map/bamij,bamjk->baik/dot_general | solution.py:54
  163.4 9.7 %exponential_reduce_fusion = f32[16,128,512]{1,2,0:T(8,128)} fusion(f32[16,2,128,512]{2,3,1,0:T(8,128)S(1)} %get-tuple-element.17, f32[16,128,512]{1,2,0:T(8,128)} %get-tuple-element.16), kind=kLoop, calls=%fused_computation.16 | loop fusion | flops 3145728 | bytes 16777216 | tf_op jit(solution)/shard_map/reduce_sum | solution.py:60
  173.1 6.0 %log_add_fusion = f32[16,128,512]{1,2,0:T(8,128)} fusion(f32[16,128,512]{1,2,0:T(8,128)} %get-tuple-element.16, f32[16,128,512]{1,2,0:T(8,128)} %exponential_reduce_fusion), kind=kLoop, calls=%fused_computation.26 | loop fusion | flops 1048576 | bytes 12582912 | tf_op jit(solution)/shard_map/add | solution.py:60
  179.1 24.5 %fusion.10 = f32[16,2,512,6,128]{4,2,3,1,0:T(8,128)} fusion(bf16[16,2,6,128,128]{4,3,2,1,0:T(8,128)(2,1)} %param.11, f32[16,2,128,512]{2,3,1,0:T(8,128)} %copy-done, f32[16,128,512]{1,2,0:T(8,128)} %log_add_fusion, f32[16,128,512]{1,2,0:T(8,128)} %copy.49), kind=kOutput, calls=%fused_computation.22 | convolution fusion | flops 3229614080 | bytes 73400320 | tf_op jit(solution)/shard_map/bamij,baik->bamjk/dot_general | solution.py:73
  203.6 4.4 %gather_fusion.2 = bf16[24,128,512]{1,2,0:T(8,128)(2,1)S(1)} fusion(f32[192,128,512]{1,2,0:T(8,128)} %bitcast.71, s32[1024]{0:T(1024)S(1)} %pad_clamp_fusion), kind=kCustom, calls=%fused_computation.2 | custom fusion | bytes 6291552 | tf_op jit(solution)/shard_map/jit(_take)/gather | solution.py:77
  208.1 2.8 copy.51
  210.9 5.0 %select_convert_fusion = bf16[4,6,128,512]{3,2,1,0:T(8,128)(2,1)} fusion(bf16[4,6,128,512]{3,2,1,0:T(8,128)(2,1)} %bitcast.78, pred[4,6]{1,0:T(4,128)(4,1)S(1)} %broadcast_in_dim.91, pred[4,6]{1,0:T(4,128)(4,1)S(1)} %broadcast_in_dim.89), kind=kLoop, calls=%fused_computation.17 | loop fusion | flops 3145728 | bytes 6291504 | tf_op jit(solution)/shard_map/convert_element_type | solution.py:78
  215.8 3.7 %all-to-all-start.2 = ((bf16[4,6,128,512]{3,2,1,0:T(8,128)(2,1)}), bf16[4,6,128,512]{3,2,1,0:T(8,128)(2,1)S(1)}, u32[]{:S(2)}, u32[]{:S(2)}) async-start(bf16[4,6,128,512]{3,2,1,0:T(8,128)(2,1)} %select_convert_fusion), calls=%async_computation.2 | async-start | bytes 6291456 | tf_op jit(solution)/shard_map/all_to_all | solution.py:79
  219.5 0.1 reshape.399
  219.6 5.3 %copy.48 = f32[16,128,512]{2,1,0:T(8,128)} copy(f32[16,128,512]{1,2,0:T(8,128)} %log_add_fusion) | data formatting | bytes 8388608 | tf_op jit(solution)/shard_map/add | solution.py:60
  225.0 49.2 %copy.50 = f32[192,128,512]{2,0,1:T(8,128)} copy(f32[192,128,512]{1,2,0:T(8,128)} %bitcast.72) | data formatting | bytes 100663296 | tf_op jit(solution)/shard_map/reshape | solution.py:75
  274.2 7.5 %fusion.7 = (f32[2,512]{1,0:T(2,128)S(1)}, f32[16,2,128]{2,1,0:T(2,128)S(1)}) fusion(f32[16,2,128,512]{2,3,1,0:T(8,128)} %copy-done, f32[16,128,512]{1,2,0:T(8,128)} %log_add_fusion, f32[16,128,512]{1,2,0:T(8,128)} %copy.49), kind=kLoop, calls=%fused_computation.18 | loop fusion | flops 8383488 | bytes 16797696 | tf_op jit(solution)/shard_map/reduce_sum | solution.py:67
  281.7 12.2 %psum.15 = f32[2,512]{1,0:T(2,128)S(1)} all-reduce(f32[2,512]{1,0:T(2,128)S(1)} %get-tuple-element.4), channel_id=1, replica_groups=mesh['groups'=2,'state'=4,'type'=4] {'state'}, use_global_device_ids=true, to_apply=%region_10.11 | all-reduce | flops 1024 | bytes 8192 | tf_op jit(solution)/shard_map/psum | solution.py:67
  293.8 10.1 %psum.14 = f32[2,2048]{1,0:T(2,128)S(1)} all-reduce(f32[2,2048]{1,0:T(2,128)S(1)} %bitcast.82), channel_id=1, replica_groups=mesh['groups'=2,'state'=4,'type'=4] {'type'}, use_global_device_ids=true, to_apply=%region_8.9 | all-reduce | flops 4096 | bytes 32768 | tf_op jit(solution)/shard_map/psum | solution.py:66
  303.9 0.6 broadcast_multiply_fusion.1
  304.5 0.6 broadcast_multiply_fusion
  305.1 23.2 %fusion.26 = f32[16,128,512]{2,0,1:T(8,128)} fusion(f32[192,128,512]{2,0,1:T(8,128)} %copy.50, s32[192]{0:T(256)S(1)} %and_select_fusion.4, pred[192]{0:T(512)(128)(4,1)S(1)} %get-tuple-element.10), kind=kOutput, calls=%fused_computation.45 | convolution fusion | flops 2415925248 | bytes 54526912 | tf_op jit(solution)/shard_map/rd,rjk->djk/dot_general | solution.py:90
  328.4 5.1 %fusion.20 = f32[16,128,512]{2,0,1:T(8,128)S(1)} fusion(f32[16,128,512]{2,0,1:T(8,128)} %fusion.26, s32[24]{0:T(128)S(1)} %reshape.399, bf16[3,8,128,512]{3,2,1,0:T(8,128)(2,1)S(1)} %bitcast.77), kind=kOutput, calls=%fused_computation.31 | convolution fusion | flops 51380608 | bytes 11534432 | tf_op jit(solution)/shard_map/dot_general | solution.py:92
  333.5 4.4 %copy.53 = f32[16,128,512]{2,1,0:T(8,128)} copy(f32[16,128,512]{2,0,1:T(8,128)S(1)} %fusion.20) | data formatting | bytes 8388608 | tf_op jit(solution)/shard_map/add | solution.py:97
  (30 shorter events, 0.4 us)
Async XLA Ops:
  23.2 74.4 %copy-start.1 = (bf16[2048,512]{1,0:T(8,128)(2,1)S(1)}, bf16[2048,512]{1,0:T(8,128)(2,1)}, u32[]{:S(2)}) copy-start(bf16[2048,512]{1,0:T(8,128)(2,1)} %param.7) | copy-start | bytes 6291460
  23.2 74.4 %all-to-all-start.1 = ((bf16[4,6,128,512]{3,2,1,0:T(8,128)(2,1)}), bf16[4,6,128,512]{3,2,1,0:T(8,128)(2,1)}, u32[]{:S(2)}, u32[]{:S(2)}) async-start(bf16[4,6,128,512]{3,2,1,0:T(8,128)(2,1)} %broadcast_select_fusion), calls=%async_computation.1 | async-start | bytes 6291456 | tf_op jit(solution)/shard_map/all_to_all | solution.py:40
  115.8 32.6 %copy-start.2 = (f32[2,2048]{1,0:T(2,128)S(1)}, f32[2,2048]{1,0:T(2,128)}, u32[]{:S(2)}) copy-start(f32[2,2048]{1,0:T(2,128)} %param.9) | copy-start | bytes 49156
  115.8 32.6 %copy-start.3 = (f32[2,512]{1,0:T(2,128)S(1)}, f32[2,512]{1,0:T(2,128)}, u32[]{:S(2)}) copy-start(f32[2,512]{1,0:T(2,128)} %param.10) | copy-start | bytes 12292
  163.4 9.7 %copy-start = (f32[16,2,128,512]{2,3,1,0:T(8,128)}, f32[16,2,128,512]{2,3,1,0:T(8,128)S(1)}, u32[]{:S(2)}) copy-start(f32[16,2,128,512]{2,3,1,0:T(8,128)S(1)} %get-tuple-element.17) | copy-start | bytes 25165828
  215.8 112.5 %all-to-all-start.2 = ((bf16[4,6,128,512]{3,2,1,0:T(8,128)(2,1)}), bf16[4,6,128,512]{3,2,1,0:T(8,128)(2,1)S(1)}, u32[]{:S(2)}, u32[]{:S(2)}) async-start(bf16[4,6,128,512]{3,2,1,0:T(8,128)(2,1)} %select_convert_fusion), calls=%async_computation.2 | async-start | bytes 6291456 | tf_op jit(solution)/shard_map/all_to_all | solution.py:79
where the time goes:
time: 340 us; the launch traced here: 338 us
  local copies, waits for them, and re-layouts  125 us (37%)
  matrix products  67.8 us (20%)
  waiting for transfers between devices  63.7 us (19%)
  other arithmetic  38.5 us (11%)
  blocking collectives  34 us (10%)
  starting transfers between devices  8.47 us (2%)
    all_to_all x1, waiting for transfers between devices, local(): lax.all_to_all(outgoing.reshape(device_count, capacity, tile_rows, type_w...  63.7 us
    reshape x1, local copies, waits for them, and re-layouts, local(): contrib = jnp.einsum('bamij,baik->bamjk', tiles, scaled, preferred_elemen...  49.2 us
    gather x2, local copies, waits for them, and re-layouts, local(): picked = jnp.take(table, lookup, axis=0)  46.1 us
    dot_general x1, matrix products, local(): jnp.einsum('bamij,baik->bamjk', tiles, scaled, preferred_element_type=jnp...  24.5 us
    dot_general x1, matrix products, local(): jnp.einsum('rd,rjk->djk', local_select, contrib, precision=lax.Precision....  23.2 us
    dot_general x1, matrix products, local(): jnp.einsum('bamij,bamjk->baik', tiles, picked, preferred_element_type=jnp...  15 us
    psum x1, blocking collectives, local(): lax.psum(jnp.sum(grad_q, axis=(0, 2)), 'state')  12.2 us
    all_to_all x1, blocking collectives, local(): lax.all_to_all(request.reshape(device_count, capacity), 'state', split_ax...  11.7 us
  transfers between devices with their start and end apart: 2, of which 1 were waited for; matrix products, arithmetic and copies ran while one was open for 27% of the time, Pallas kernels for 0%

commit v1 on v0

--- a/solution.py
+++ b/solution.py
@@ -2,6 +2,32 @@
 import jax.numpy as jnp
 from jax import lax
 from jax.sharding import PartitionSpec as P
+
+
+def plate_load(w_in, array_dim, in_array):
+    mixed_arr, mid_arr = (w_in.shape[:array_dim], w_in.shape[array_dim + 1 :])
+    return jnp.moveaxis(w_in.reshape(*mixed_arr, in_array, -1, *mid_arr), array_dim, 0)
+
+
+def _pass_tiles(here_x, pos_dim):
+    here_x = jnp.moveaxis(here_x, 0, pos_dim)
+    frame_out = here_x.shape
+    return here_x.reshape(
+        *frame_out[:pos_dim], frame_out[pos_dim] * frame_out[pos_dim + 1], *frame_out[pos_dim + 2 :]
+    )
+
+
+def map_rows(field_in, comm_axis, incoming_x, z_in):
+    z, new = (lax.axis_size(comm_axis), lax.axis_index(comm_axis))
+    arr_out = plate_load(field_in, incoming_x, z)
+    slots = [arr_out[new]]
+    w = 1
+    while w < z:
+        local_now = arr_out[new ^ w]
+        slots.append(lax.ppermute(local_now, comm_axis, [(dev_j, dev_j ^ w) for dev_j in range(z)]))
+        w = w + 1
+    arr_out = jnp.stack(slots)[new ^ jnp.arange(z)]
+    return _pass_tiles(arr_out, z_in)
 
 
 def local(value_in, cotangent, state_util, taste, tiles, dest_block, counts):
@@ -37,12 +63,8 @@
         request.reshape(device_count, capacity), "state", split_axis=0, concat_axis=0, tiled=True
     )
     outgoing = jnp.take(value_blocks, jnp.clip(wanted.reshape(-1), 0, block_count - 1), axis=0)
-    incoming = lax.all_to_all(
-        outgoing.reshape(device_count, capacity, tile_rows, type_width),
-        "state",
-        split_axis=0,
-        concat_axis=0,
-        tiled=True,
+    incoming = map_rows(
+        outgoing.reshape(device_count, capacity, tile_rows, type_width), "state", 0, 0
     )
     table = jnp.concatenate(
         [value_blocks, incoming.reshape(device_count * capacity, tile_rows, type_width)], axis=0

time: 340 us -> 343 us (level)
  blocking collectives: 34 us -> 22.3 us
  starting transfers between devices: 8.47 us -> 14.4 us
  local copies, waits for them, and re-layouts: 125 us -> 130 us
    ppermute x0 -> x3, waiting for transfers between devices: none -> 61 us  [map_rows(): lax.ppermute(local_now, comm_axis, [(dev_j, dev_j ^ w) for dev_j in range...]
    all_to_all x1, waiting for transfers between devices: 63.7 us -> 4.15 us  [local(): lax.all_to_all(request.reshape(device_count, capacity), 'state', split_ax...]
    all_to_all x1 -> x0, blocking collectives: 11.7 us -> none  [local(): lax.all_to_all(request.reshape(device_count, capacity), 'state', split_ax...]
    gather x0 -> x1, local copies, waits for them, and re-layouts: none -> 4.45 us  [map_rows(): arr_out = jnp.stack(slots)[new ^ jnp.arange(z)]]
    ppermute x0 -> x3, starting transfers between devices: none -> 4.39 us  [map_rows(): lax.ppermute(local_now, comm_axis, [(dev_j, dev_j ^ w) for dev_j in range...]
  transfers between devices with their start and end apart: 2 -> 5, of which waited for: 1 -> 3; matrix products, arithmetic and copies ran while one was open for 27% -> 27% of each run, Pallas kernels for 0% -> 0%
where the time goes in v1:
time: 343 us; the launch traced here: 340 us
  local copies, waits for them, and re-layouts  130 us (38%)
  matrix products  67.8 us (20%)
  waiting for transfers between devices  65.2 us (19%)
  other arithmetic  39.9 us (12%)
  blocking collectives  22.3 us (7%)
  starting transfers between devices  14.4 us (4%)
    ppermute x3, waiting for transfers between devices, map_rows(): lax.ppermute(local_now, comm_axis, [(dev_j, dev_j ^ w) for dev_j in range...  61 us
    reshape x1, local copies, waits for them, and re-layouts, local(): contrib = jnp.einsum('bamij,baik->bamjk', tiles, scaled, preferred_elemen...  49.2 us
    gather x2, local copies, waits for them, and re-layouts, local(): picked = jnp.take(table, lookup, axis=0)  46.1 us
    dot_general x1, matrix products, local(): jnp.einsum('bamij,baik->bamjk', tiles, scaled, preferred_element_type=jnp...  24.5 us
    dot_general x1, matrix products, local(): jnp.einsum('rd,rjk->djk', local_select, contrib, precision=lax.Precision....  23.2 us
    dot_general x1, matrix products, local(): jnp.einsum('bamij,bamjk->baik', tiles, picked, preferred_element_type=jnp...  15 us
    psum x1, blocking collectives, local(): lax.psum(jnp.sum(grad_q, axis=(0, 2)), 'state')  12.2 us
    psum x1, blocking collectives, local(): lax.psum(util_part, 'type') / (type_width * lax.axis_size('type'))  10.1 us
  transfers between devices with their start and end apart: 5, of which 3 were waited for; matrix products, arithmetic and copies ran while one was open for 27% of the time, Pallas kernels for 0%

profile of v1, /device:TPU:0, one launch (start us, length us, event | category | flops | bytes accessed | tf_op | source)
XLA Modules:
  0.0 340.4 jit_solution(16940988382889361916)
XLA Ops:
  0.6 0.8 copy.37
  1.5 0.1 lt.128
  1.6 0.1 lt.131
  1.7 0.8 copy.38
  2.5 0.1 reshape.415
  2.6 0.1 reshape.419
  2.8 1.2 reduce-window.6
  4.5 1.2 scatter_custom_fusion
  5.7 0.7 all_to_all.9
  6.4 6.3 %all-to-all-start = ((s32[4,1,6]{2,1,0:T(1,128)}), s32[4,1,6]{2,1,0:T(1,128)S(1)}, u32[]{:S(2)}, u32[]{:S(2)}) async-start(s32[4,1,6]{2,1,0:T(1,128)} %bitcast.7), calls=%async_computation | async-start | bytes 4096 | tf_op jit(solution)/shard_map/all_to_all | solution.py:62
  12.7 0.1 reduce_sum.41
  12.8 1.2 scatter_custom_fusion.1
  14.1 4.1 %all-to-all-done = s32[4,1,6]{2,1,0:T(1,128)S(1)} async-done(((s32[4,1,6]{2,1,0:T(1,128)}), s32[4,1,6]{2,1,0:T(1,128)S(1)}, u32[]{:S(2)}, u32[]{:S(2)}) %all-to-all-start) | async-done | bytes 128 | tf_op jit(solution)/shard_map/all_to_all | solution.py:62
  18.2 0.5 broadcast.565
  18.7 0.7 fusion.48
  19.5 2.3 gather_fusion
  21.9 0.4 broadcast_select_fusion
  22.2 1.5 constant_dynamic-slice_fusion
  23.7 0.6 collective-permute-start.2
  24.3 1.5 collective-permute-start.1
  25.8 2.4 collective-permute-start
  28.3 3.0 copy.49
  31.3 0.1 compare_and_fusion
  31.4 14.9 %collective-permute-done.2 = bf16[1,6,128,512]{3,2,1,0:T(8,128)(2,1)} collective-permute-done((bf16[1,6,128,512]{3,2,1,0:T(8,128)(2,1)}, bf16[1,6,128,512]{3,2,1,0:T(8,128)(2,1)}, u32[]{:S(2)}, u32[]{:S(2)}) %collective-permute-start.2) | collective-permute-done | bytes 786464 | tf_op jit(solution)/shard_map/ppermute | solution.py:27
  46.4 46.1 %collective-permute-done.1 = bf16[1,6,128,512]{3,2,1,0:T(8,128)(2,1)} collective-permute-done((bf16[1,6,128,512]{3,2,1,0:T(8,128)(2,1)}, bf16[1,6,128,512]{3,2,1,0:T(8,128)(2,1)}, u32[]{:S(2)}, u32[]{:S(2)}) %collective-permute-start.1) | collective-permute-done | bytes 786464 | tf_op jit(solution)/shard_map/ppermute | solution.py:27
  92.5 3.1 maximum_bitcast_fusion
  95.6 4.4 %gather_fusion.1 = bf16[4,6,128,512]{3,2,1,0:T(8,128)(2,1)} fusion(bf16[4,6,128,512]{3,2,1,0:T(8,128)(2,1)} %maximum_bitcast_fusion, s32[1024]{0:T(1024)S(1)} %pad_clamp_fusion.2), kind=kCustom, calls=%fused_computation.1 | custom fusion | bytes 6291472 | tf_op jit(solution)/shard_map/gather | solution.py:29
  100.0 4.7 %pad_maximum_fusion = bf16[40,128,512]{2,1,0:T(8,128)(2,1)} fusion(bf16[24,128,512]{2,1,0:T(8,128)(2,1)} %bitcast.92, bf16[16,128,512]{2,1,0:T(8,128)(2,1)S(1)} %bitcast.88), kind=kLoop, calls=%fused_computation.21 | loop fusion | flops 2621440 | bytes 10485760 | tf_op jit(solution)/shard_map/concatenate | solution.py:69
  104.7 13.6 %gather_fusion.2 = bf16[192,128,512]{2,1,0:T(8,128)(2,1)} fusion(bf16[40,128,512]{2,1,0:T(8,128)(2,1)} %pad_maximum_fusion, s32[1024]{0:T(1024)S(1)} %pad_clamp_fusion.1), kind=kCustom, calls=%fused_computation.2 | custom fusion | bytes 50332416 | tf_op jit(solution)/shard_map/jit(_take)/gather | solution.py:73
  118.3 32.6 %copy.47 = bf16[16,2,6,128,512]{3,4,2,1,0:T(8,128)(2,1)} copy(bf16[16,2,6,128,512]{4,3,2,1,0:T(8,128)(2,1)} %bitcast.86) | data formatting | bytes 50331648 | tf_op jit(solution)/shard_map/jit(_take)/gather | solution.py:73
  150.9 15.0 %fusion.49 = (f32[16,128,512]{1,2,0:T(8,128)}, f32[16,2,128,512]{2,3,1,0:T(8,128)S(1)}) fusion(bf16[16,2,6,128,128]{4,3,2,1,0:T(8,128)(2,1)} %param.11, bf16[16,2,6,128,512]{3,4,2,1,0:T(8,128)(2,1)} %copy.47, pred[16,2,6]{2,1,0:T(4,128)(4,1)S(1)} %compare_and_fusion, pred[16,2,6]{2,1,0:T(4,128)(4,1)S(1)} %iota_compare_fusion.1, ...), kind=kOutput, calls=%fused_computation.111 | convolution fusion | flops 3253731328 | bytes 44061056 | tf_op jit(solution)/shard_map/bamij,bamjk->baik/dot_general | solution.py:76
  165.8 9.7 %exponential_reduce_fusion = f32[16,128,512]{1,2,0:T(8,128)} fusion(f32[16,2,128,512]{2,3,1,0:T(8,128)S(1)} %get-tuple-element.21, f32[16,128,512]{1,2,0:T(8,128)} %get-tuple-element.20), kind=kLoop, calls=%fused_computation.17 | loop fusion | flops 3145728 | bytes 16777216 | tf_op jit(solution)/shard_map/reduce_sum | solution.py:82
  175.6 6.0 %log_add_fusion = f32[16,128,512]{1,2,0:T(8,128)} fusion(f32[16,128,512]{1,2,0:T(8,128)} %get-tuple-element.20, f32[16,128,512]{1,2,0:T(8,128)} %exponential_reduce_fusion), kind=kLoop, calls=%fused_computation.27 | loop fusion | flops 1048576 | bytes 12582912 | tf_op jit(solution)/shard_map/add | solution.py:82
  181.6 24.5 %fusion.10 = f32[16,2,512,6,128]{4,2,3,1,0:T(8,128)} fusion(bf16[16,2,6,128,128]{4,3,2,1,0:T(8,128)(2,1)} %param.11, f32[16,2,128,512]{2,3,1,0:T(8,128)} %copy-done, f32[16,128,512]{1,2,0:T(8,128)} %log_add_fusion, f32[16,128,512]{1,2,0:T(8,128)} %copy.49), kind=kOutput, calls=%fused_computation.23 | convolution fusion | flops 3229614080 | bytes 73400320 | tf_op jit(solution)/shard_map/bamij,baik->bamjk/dot_general | solution.py:95
  206.1 4.4 %gather_fusion.3 = bf16[24,128,512]{1,2,0:T(8,128)(2,1)S(1)} fusion(f32[192,128,512]{1,2,0:T(8,128)} %bitcast.84, s32[1024]{0:T(1024)S(1)} %pad_clamp_fusion), kind=kCustom, calls=%fused_computation.3 | custom fusion | bytes 6291552 | tf_op jit(solution)/shard_map/jit(_take)/gather | solution.py:99
  210.6 2.8 copy.51
  213.3 5.0 %select_convert_fusion = bf16[4,6,128,512]{3,2,1,0:T(8,128)(2,1)} fusion(bf16[4,6,128,512]{3,2,1,0:T(8,128)(2,1)} %bitcast.91, pred[4,6]{1,0:T(4,128)(4,1)S(1)} %broadcast_in_dim.92, pred[4,6]{1,0:T(4,128)(4,1)S(1)} %broadcast_in_dim.90), kind=kLoop, calls=%fused_computation.18 | loop fusion | flops 3145728 | bytes 6291504 | tf_op jit(solution)/shard_map/convert_element_type | solution.py:100
  218.3 3.7 %all-to-all-start.1 = ((bf16[4,6,128,512]{3,2,1,0:T(8,128)(2,1)}), bf16[4,6,128,512]{3,2,1,0:T(8,128)(2,1)S(1)}, u32[]{:S(2)}, u32[]{:S(2)}) async-start(bf16[4,6,128,512]{3,2,1,0:T(8,128)(2,1)} %select_convert_fusion), calls=%async_computation.1 | async-start | bytes 6291456 | tf_op jit(solution)/shard_map/all_to_all | solution.py:101
  222.1 5.3 %copy.48 = f32[16,128,512]{2,1,0:T(8,128)} copy(f32[16,128,512]{1,2,0:T(8,128)} %log_add_fusion) | data formatting | bytes 8388608 | tf_op jit(solution)/shard_map/add | solution.py:82
  227.4 49.2 %copy.50 = f32[192,128,512]{2,0,1:T(8,128)} copy(f32[192,128,512]{1,2,0:T(8,128)} %bitcast.85) | data formatting | bytes 100663296 | tf_op jit(solution)/shard_map/reshape | solution.py:97
  276.6 7.5 %fusion.7 = (f32[2,512]{1,0:T(2,128)S(1)}, f32[16,2,128]{2,1,0:T(2,128)S(1)}) fusion(f32[16,2,128,512]{2,3,1,0:T(8,128)} %copy-done, f32[16,128,512]{1,2,0:T(8,128)} %log_add_fusion, f32[16,128,512]{1,2,0:T(8,128)} %copy.49), kind=kLoop, calls=%fused_computation.19 | loop fusion | flops 8383488 | bytes 16797696 | tf_op jit(solution)/shard_map/reduce_sum | solution.py:89
  284.1 12.2 %psum.15 = f32[2,512]{1,0:T(2,128)S(1)} all-reduce(f32[2,512]{1,0:T(2,128)S(1)} %get-tuple-element.4), channel_id=1, replica_groups=mesh['groups'=2,'state'=4,'type'=4] {'state'}, use_global_device_ids=true, to_apply=%region_10.11 | all-reduce | flops 1024 | bytes 8192 | tf_op jit(solution)/shard_map/psum | solution.py:89
  296.3 10.1 %psum.14 = f32[2,2048]{1,0:T(2,128)S(1)} all-reduce(f32[2,2048]{1,0:T(2,128)S(1)} %bitcast.96), channel_id=1, replica_groups=mesh['groups'=2,'state'=4,'type'=4] {'type'}, use_global_device_ids=true, to_apply=%region_8.9 | all-reduce | flops 4096 | bytes 32768 | tf_op jit(solution)/shard_map/psum | solution.py:88
  306.4 0.6 broadcast_multiply_fusion.1
  307.0 0.6 broadcast_multiply_fusion
  307.6 23.2 %fusion.26 = f32[16,128,512]{2,0,1:T(8,128)} fusion(f32[192,128,512]{2,0,1:T(8,128)} %copy.50, s32[192]{0:T(256)S(1)} %and_select_fusion.4, pred[192]{0:T(512)(128)(4,1)S(1)} %get-tuple-element.10), kind=kOutput, calls=%fused_computation.50 | convolution fusion | flops 2415925248 | bytes 54526912 | tf_op jit(solution)/shard_map/rd,rjk->djk/dot_general | solution.py:112
  330.9 5.1 %fusion.20 = f32[16,128,512]{2,0,1:T(8,128)S(1)} fusion(f32[16,128,512]{2,0,1:T(8,128)} %fusion.26, s32[24]{0:T(128)S(1)} %reshape.421, bf16[3,8,128,512]{3,2,1,0:T(8,128)(2,1)S(1)} %bitcast.90), kind=kOutput, calls=%fused_computation.33 | convolution fusion | flops 51380608 | bytes 11534432 | tf_op jit(solution)/shard_map/dot_general | solution.py:114
  335.9 4.4 %copy.53 = f32[16,128,512]{2,1,0:T(8,128)} copy(f32[16,128,512]{2,0,1:T(8,128)S(1)} %fusion.20) | data formatting | bytes 8388608 | tf_op jit(solution)/shard_map/add | solution.py:119
  (42 shorter events, 1.0 us)
Async XLA Ops:
  6.4 11.8 %all-to-all-start = ((s32[4,1,6]{2,1,0:T(1,128)}), s32[4,1,6]{2,1,0:T(1,128)S(1)}, u32[]{:S(2)}, u32[]{:S(2)}) async-start(s32[4,1,6]{2,1,0:T(1,128)} %bitcast.7), calls=%async_computation | async-start | bytes 4096 | tf_op jit(solution)/shard_map/all_to_all | solution.py:62
  22.2 6.1 %copy-start.2 = (bf16[2048,512]{1,0:T(8,128)(2,1)S(1)}, bf16[2048,512]{1,0:T(8,128)(2,1)}, u32[]{:S(2)}) copy-start(bf16[2048,512]{1,0:T(8,128)(2,1)} %param.8) | copy-start | bytes 6291460
  23.7 22.6 %collective-permute-start.2 = (bf16[1,6,128,512]{3,2,1,0:T(8,128)(2,1)}, bf16[1,6,128,512]{3,2,1,0:T(8,128)(2,1)}, u32[]{:S(2)}, u32[]{:S(2)}) collective-permute-start(bf16[1,6,128,512]{3,2,1,0:T(8,128)(2,1)} %get-tuple-element.15), channel_id=1, source_target_pairs={{0,12},{4,8},{8,4},{12,0},{1,13},{5,9},{9,5},{13,1},{2,14},{6,10},... | collective-permute-start | bytes 2359304 | tf_op jit(solution)/shard_map/ppermute | solution.py:27
  24.3 68.2 %collective-permute-start.1 = (bf16[1,6,128,512]{3,2,1,0:T(8,128)(2,1)}, bf16[1,6,128,512]{3,2,1,0:T(8,128)(2,1)}, u32[]{:S(2)}, u32[]{:S(2)}) collective-permute-start(bf16[1,6,128,512]{3,2,1,0:T(8,128)(2,1)} %get-tuple-element.16), channel_id=1, source_target_pairs={{0,8},{4,12},{8,0},{12,4},{1,9},{5,13},{9,1},{13,5},{2,10},{6,14},... | collective-permute-start | bytes 2359304 | tf_op jit(solution)/shard_map/ppermute | solution.py:27
  25.8 66.7 %collective-permute-start = (bf16[1,6,128,512]{3,2,1,0:T(8,128)(2,1)}, bf16[1,6,128,512]{3,2,1,0:T(8,128)(2,1)}, u32[]{:S(2)}, u32[]{:S(2)}) collective-permute-start(bf16[1,6,128,512]{3,2,1,0:T(8,128)(2,1)} %get-tuple-element.17), channel_id=1, source_target_pairs={{0,4},{4,0},{8,12},{12,8},{1,5},{5,1},{9,13},{13,9},{2,6},{6,2},{1... | collective-permute-start | bytes 2359304 | tf_op jit(solution)/shard_map/ppermute | solution.py:27
  95.6 4.5 %copy-start.1 = (bf16[2048,512]{1,0:T(8,128)(2,1)S(1)}, bf16[2048,512]{1,0:T(8,128)(2,1)}, u32[]{:S(2)}) copy-start(bf16[2048,512]{1,0:T(8,128)(2,1)} %param.7) | copy-start | bytes 6291460
  118.3 32.6 %copy-start.3 = (f32[2,2048]{1,0:T(2,128)S(1)}, f32[2,2048]{1,0:T(2,128)}, u32[]{:S(2)}) copy-start(f32[2,2048]{1,0:T(2,128)} %param.9) | copy-start | bytes 49156
  118.3 32.6 %copy-start.4 = (f32[2,512]{1,0:T(2,128)S(1)}, f32[2,512]{1,0:T(2,128)}, u32[]{:S(2)}) copy-start(f32[2,512]{1,0:T(2,128)} %param.10) | copy-start | bytes 12292
  165.8 9.7 %copy-start = (f32[16,2,128,512]{2,3,1,0:T(8,128)}, f32[16,2,128,512]{2,3,1,0:T(8,128)S(1)}, u32[]{:S(2)}) copy-start(f32[16,2,128,512]{2,3,1,0:T(8,128)S(1)} %get-tuple-element.21) | copy-start | bytes 25165828
  218.3 112.5 %all-to-all-start.1 = ((bf16[4,6,128,512]{3,2,1,0:T(8,128)(2,1)}), bf16[4,6,128,512]{3,2,1,0:T(8,128)(2,1)S(1)}, u32[]{:S(2)}, u32[]{:S(2)}) async-start(bf16[4,6,128,512]{3,2,1,0:T(8,128)(2,1)} %select_convert_fusion), calls=%async_computation.1 | async-start | bytes 6291456 | tf_op jit(solution)/shard_map/all_to_all | solution.py:101
